TPU v7x, 256 devices: a whole 4x4x8 slice. The times are simulated.
256 devices in a mesh: space: 32 (over x, y, core), tm: 8 (over z).
Axes of the slice: x: 4, y: 4, z: 8, core: 2. Of those that a mesh axis runs over, the one named last changes fastest.
Arguments:
- velocity: bfloat16 [256, 2, 512, 1024], P('tm', None, 'space'), may hold values from -8.4 to 8.4
Outputs:
- vorticity: bfloat16 [256, 512, 1024], P('tm', 'space')
- modes: float32 [32, 512, 1024], P('tm', 'space')
All inputs are finite; a program needn't handle non-finite values.
Results may differ from a plain program's by a relative error of at most 0.003.
Values may be sent and summed in bfloat16 or wider, within the bound.
A program may use at most 64 MiB of HBM per device.

v0:
```python
import jax
import jax.numpy as jnp
from jax import lax
from jax.sharding import PartitionSpec as P

RANK = 32
HIGH = lax.Precision.HIGHEST


def halo_rows(block, width):
    count = lax.axis_size("space")
    forward = [(i, (i + 1) % count) for i in range(count)]
    backward = [(target, source) for source, target in forward]
    rows = block.shape[1]
    low = lax.ppermute(block[:, rows - width :], "space", forward)
    high = lax.ppermute(block[:, :width], "space", backward)
    return jnp.concatenate([low, block, high], axis=1)


def spanwise(field):
    ahead = jnp.roll(field, -1, 2)
    behind = jnp.roll(field, 1, 2)
    ahead_two = jnp.roll(field, -2, 2)
    behind_two = jnp.roll(field, 2, 2)
    return (8.0 * (ahead - behind) - (ahead_two - behind_two)) / 12.0


def merge_small(gram):
    coeffs = gram[:, :, :RANK] + gram[:, :, RANK:]
    diagonal = jnp.diagonal(gram, axis1=1, axis2=2)
    scales = jnp.sqrt(diagonal[:, :RANK] + diagonal[:, RANK:])
    half = jnp.einsum("nab,nbc->nac", gram, coeffs, precision=HIGH)
    inner = jnp.einsum("nab,nac->nbc", coeffs, half, precision=HIGH)
    lower = jnp.linalg.cholesky(inner)
    eye = jnp.broadcast_to(jnp.eye(RANK, dtype=jnp.float32), inner.shape)
    lower_inv = lax.linalg.triangular_solve(lower, eye, left_side=True, lower=True)
    factor = jnp.swapaxes(lower_inv, 1, 2) * scales[:, None, :]
    return jnp.einsum("nab,nbc->nac", coeffs, factor, precision=HIGH)


def tree_basis(gram, leaves):
    width = leaves * RANK
    basis = None
    span = 1
    while span < leaves:
        nodes = leaves // (2 * span)
        size = 2 * span * RANK
        sub = jnp.stack(
            [gram[k * size : (k + 1) * size, k * size : (k + 1) * size] for k in range(nodes)]
        )
        if basis is None:
            h = sub
        else:
            b = basis.reshape(nodes, 2, span * RANK, RANK)
            zero = jnp.zeros_like(b[:, 0])
            bd = jnp.concatenate(
                [
                    jnp.concatenate([b[:, 0], zero], axis=2),
                    jnp.concatenate([zero, b[:, 1]], axis=2),
                ],
                axis=1,
            )
            gb = jnp.einsum("nab,nbc->nac", sub, bd, precision=HIGH)
            h = jnp.einsum("nab,nac->nbc", bd, gb, precision=HIGH)
        c = merge_small(h)
        if basis is None:
            basis = c
        else:
            basis = jnp.einsum("nab,nbc->nac", bd, c, precision=HIGH)
        span *= 2
    return basis.reshape(width, RANK)


def local(velocity):
    rows = velocity.shape[2]
    span_v = halo_rows(velocity[:, 1], 2).astype(jnp.float32)
    stream_u = velocity[:, 0].astype(jnp.float32)
    dv_dx = (
        8.0 * (span_v[:, 3 : rows + 3] - span_v[:, 1 : rows + 1])
        - (span_v[:, 4:] - span_v[:, :rows])
    ) / 12.0
    vorticity = (dv_dx - spanwise(stream_u)).astype(jnp.bfloat16)
    blocks = lax.axis_size("tm")
    cells = lax.all_to_all(vorticity, "tm", 2, 0, tiled=True)
    flat = cells.reshape(cells.shape[0], -1)
    gram = jnp.einsum("ax,bx->ab", flat, flat, preferred_element_type=jnp.float32)
    gram = lax.psum(gram, ("space", "tm"))
    basis = tree_basis(gram, blocks)
    part = jnp.einsum("ab,ax->bx", basis, flat.astype(jnp.float32), precision=HIGH).reshape(
        RANK, rows, -1
    )
    modes = lax.all_to_all(part, "tm", 0, 2, tiled=True)
    return (vorticity, modes)


def solution(mesh):
    in_specs = (P("tm", None, "space", None),)
    out_specs = (P("tm", "space", None), P("tm", "space", None))
    return jax.shard_map(local, mesh=mesh, in_specs=in_specs, out_specs=out_specs, check_vma=False)
```

profile of v0, /device:TPU:2, one launch (start us, length us, event | category | flops | bytes accessed | tf_op | source)
XLA Modules:
  0.0 411.2 jit_solution(9131504356403751906)
XLA Ops:
  7.2 1.9 bitcast_convert_fusion
  9.0 0.6 copy.179
  9.7 3.8 collective-permute-start.1
  13.6 0.7 fusion.72
  14.3 0.7 fusion.74
  15.4 0.8 collective-permute-done
  16.4 0.8 copy_convert_fusion
  17.2 2.2 fusion.3
  19.4 5.1 %copy.130 = bf16[32,16,1024]{0,1,2:T(8,128)(2,1)} copy(bf16[32,16,1024]{2,1,0:T(8,128)(2,1)S(1)} %fusion.3) | data formatting | bytes 2097152 | tf_op jit(solution)/shard_map/convert_element_type | solution.py:82
  24.5 7.8 %reshape.157 = bf16[8,2,32768]{2,1,0:T(2,128)(2,1)} reshape(bf16[1024,16,32]{2,1,0:T(8,128)(2,1)} %bitcast.133) | data formatting | bytes 2097152
  32.4 8.5 %all-to-all-start = ((bf16[8,2,32768]{2,1,0:T(2,128)(2,1)}), bf16[8,2,32768]{2,1,0:T(2,128)(2,1)S(1)}, u32[]{:S(2)}, u32[]{:S(2)}) async-start(bf16[8,2,32768]{2,1,0:T(2,128)(2,1)} %reshape.157), calls=%async_computation | async-start | bytes 2097152 | tf_op jit(solution)/shard_map/all_to_all | solution.py:84
  41.1 28.5 %all-to-all-done = bf16[8,2,32768]{2,1,0:T(2,128)(2,1)S(1)} async-done(((bf16[8,2,32768]{2,1,0:T(2,128)(2,1)}), bf16[8,2,32768]{2,1,0:T(2,128)(2,1)S(1)}, u32[]{:S(2)}, u32[]{:S(2)}) %all-to-all-start) | async-done | bytes 1048608 | tf_op jit(solution)/shard_map/all_to_all | solution.py:84
  69.6 4.5 %reshape.158 = bf16[1024,16,32]{2,1,0:T(8,128)(2,1)} reshape(bf16[8,2,32768]{2,1,0:T(2,128)(2,1)S(1)} %all-to-all-done) | data formatting | bytes 2097152
  74.1 5.4 %copy.131 = bf16[32,16,8,128]{3,1,0,2:T(8,128)(2,1)S(1)} copy(bf16[32,16,8,128]{0,1,3,2:T(8,128)(2,1)} %bitcast.132) | data formatting | bytes 2097152 | tf_op jit(solution)/shard_map/all_to_all | solution.py:84
  79.5 1.2 fusion.10
  80.7 0.7 copy.133
  81.4 0.3 copy.178
  81.7 0.5 copy.152
  82.2 244.6 %all-reduce.6.cloned.1.call-done = f32[256,256]{0,1:T(8,128)} async-done(((f32[256,256]{0,1:T(8,128)}), f32[256,256]{0,1:T(8,128)}) %all-reduce.6.cloned.1.call-update) | async-done | bytes 262160 | tf_op jit(solution)/shard_map/psum | solution.py:87
  326.8 0.9 slice_bitcast_fusion.7
  327.8 1.9 copy.137
  329.7 0.9 fusion.70
  330.6 1.5 gather_fusion
  332.0 0.8 copy.138
  332.9 1.1 fusion.69
  334.1 11.7 %custom-call.21 = f32[4,32,32]{2,1,0:T(8,128)S(1)} custom-call(f32[4,32,32]{2,1,0:T(8,128)S(1)} %fusion.19), custom_call_target="Cholesky" | custom-call | tf_op jit(solution)/shard_map/jit(cholesky)/cholesky | solution.py:34
  346.1 9.8 %custom-call.22 = f32[4,1,32,32]{2,3,1,0:T(8,128)S(1)} custom-call(f32[4,1,32,32]{3,2,1,0:T(8,128)S(1)} %select_bitcast_fusion), custom_call_target="InvertDiagBlocksLowerTriangular" | custom-call | tf_op jit(solution)/shard_map/triangular_solve | solution.py:36
  355.9 0.9 convolution_multiply_fusion
  356.9 0.3 fusion.68
  357.2 0.3 fusion.13
  357.5 0.3 fusion.39
  357.8 1.9 copy.147
  359.7 0.8 fusion.67
  360.5 1.5 gather_fusion.1
  362.0 0.8 copy.148
  362.9 0.9 fusion.66
  363.9 5.9 %custom-call.23 = f32[2,32,32]{2,1,0:T(8,128)S(1)} custom-call(f32[2,32,32]{2,1,0:T(8,128)S(1)} %fusion.32), custom_call_target="Cholesky" | custom-call | tf_op jit(solution)/shard_map/jit(cholesky)/cholesky | solution.py:34
  370.0 4.9 %custom-call.24 = f32[2,1,32,32]{2,3,1,0:T(8,128)S(1)} custom-call(f32[2,1,32,32]{3,2,1,0:T(8,128)S(1)} %select_bitcast_fusion.1), custom_call_target="InvertDiagBlocksLowerTriangular" | custom-call | tf_op jit(solution)/shard_map/triangular_solve | solution.py:36
  375.0 0.9 convolution_multiply_fusion.1
  376.4 0.3 fusion.23
  376.9 0.8 gather_fusion.2
  378.1 2.9 custom-call.25
  381.0 0.6 compare_reduce_fusion
  381.7 0.7 fusion.34
  382.3 2.4 custom-call.26
  385.4 1.0 fusion.76
  386.6 17.1 %all_to_all.33 = f32[32,16,128]{2,1,0:T(8,128)S(1)} all-to-all(f32[32,16,128]{2,1,0:T(8,128)S(1)} %copy.153), channel_id=1, replica_groups=mesh['space'=32,'tm'=8] {'tm'}, dimensions={0} | all-to-all | bytes 524288 | tf_op jit(solution)/shard_map/all_to_all | solution.py:92
  403.7 0.7 copy.180
  (45 shorter events, 3.5 us)
Async XLA Ops:
  9.6 6.6 %collective-permute-start = (bf16[32,2,1024]{2,0,1:T(8,128)(2,1)S(1)}, bf16[32,2,1024]{2,0,1:T(8,128)(2,1)S(1)}, u32[]{:S(2)}, u32[]{:S(2)}) collective-permute-start(bf16[32,2,1024]{2,0,1:T(8,128)(2,1)S(1)} %get-tuple-element.18), channel_id=1, source_target_pairs={{0,8},{8,16},{16,24},{24,32},{32,40},{40,48},{48,56},{56,64},{64,7... | collective-permute-start | bytes 393224 | tf_op jit(solution)/shard_map/ppermute | solution.py:15
  9.7 6.5 %collective-permute-start.1 = (bf16[32,2,1024]{2,0,1:T(8,128)(2,1)S(1)}, bf16[32,2,1024]{2,0,1:T(8,128)(2,1)S(1)}, u32[]{:S(2)}, u32[]{:S(2)}) collective-permute-start(bf16[32,2,1024]{2,0,1:T(8,128)(2,1)S(1)} %get-tuple-element.19), channel_id=1, source_target_pairs={{8,0},{16,8},{24,16},{32,24},{40,32},{48,40},{56,48},{64,56},{72,6... | collective-permute-start | bytes 393224 | tf_op jit(solution)/shard_map/ppermute | solution.py:16
  19.4 5.1 %copy-start = (bf16[32,16,1024]{2,1,0:T(8,128)(2,1)}, bf16[32,16,1024]{2,1,0:T(8,128)(2,1)S(1)}, u32[]{:S(2)}) copy-start(bf16[32,16,1024]{2,1,0:T(8,128)(2,1)S(1)} %fusion.3) | copy-start | bytes 3145732
  32.4 37.2 %all-to-all-start = ((bf16[8,2,32768]{2,1,0:T(2,128)(2,1)}), bf16[8,2,32768]{2,1,0:T(2,128)(2,1)S(1)}, u32[]{:S(2)}, u32[]{:S(2)}) async-start(bf16[8,2,32768]{2,1,0:T(2,128)(2,1)} %reshape.157), calls=%async_computation | async-start | bytes 2097152 | tf_op jit(solution)/shard_map/all_to_all | solution.py:84
  40.8 286.0 %all-reduce.6.cloned.1.call-start = ((), (), s32[]{:S(2)}) async-start(), calls=%async_computation.2 | async-start | bytes 524288 | tf_op jit(solution)/shard_map/psum | solution.py:87
  327.7 29.5 %copy-start.1 = (f32[256,256]{0,1:T(8,128)S(1)}, f32[256,256]{0,1:T(8,128)}, u32[]{:S(2)}) copy-start(f32[256,256]{0,1:T(8,128)} %all-reduce.6.cloned.1.call-done) | copy-start | bytes 786436
Sparse Core Ops, SparseCore 0:
  80.8 245.9 all-reduce.5
where the time goes:
time: 412 us; the launch traced here: 411 us
  waiting for transfers between devices  274 us (67%)
  other arithmetic  44.8 us (11%)
  local copies, waits for them, and re-layouts  37.9 us (9%)
  blocking collectives  17.1 us (4%)
  between operations  14.4 us (3%)
  starting transfers between devices  12.6 us (3%)
  matrix products  10.4 us (3%)
    psum x1, waiting for transfers between devices, local(): gram = lax.psum(gram, ('space', 'tm'))  245 us
    all_to_all x1, waiting for transfers between devices, local(): cells = lax.all_to_all(vorticity, 'tm', 2, 0, tiled=True)  28.5 us
    another operation x9, other arithmetic, merge_small(): lower = jnp.linalg.cholesky(inner)  21.5 us
    another operation x7, other arithmetic, merge_small(): lax.linalg.triangular_solve(lower, eye, left_side=True, lower=True)  18 us
    all_to_all x1, blocking collectives, local(): modes = lax.all_to_all(part, 'tm', 0, 2, tiled=True)  17.1 us
    unnamed x8, local copies, waits for them, and re-layouts  13.2 us
    all_to_all x1, starting transfers between devices, local(): cells = lax.all_to_all(vorticity, 'tm', 2, 0, tiled=True)  8.47 us
  transfers between devices with their start and end apart: 4, of which 3 were waited for; matrix products, arithmetic and copies ran while one was open for 1% of the time, Pallas kernels for 0%

commit v1 on v0

--- a/solution.py
+++ b/solution.py
@@ -84,7 +84,8 @@
     cells = lax.all_to_all(vorticity, "tm", 2, 0, tiled=True)
     flat = cells.reshape(cells.shape[0], -1)
     gram = jnp.einsum("ax,bx->ab", flat, flat, preferred_element_type=jnp.float32)
-    gram = lax.psum(gram, ("space", "tm"))
+    for name in ("space", "tm"):
+        gram = lax.psum(gram, name)
     basis = tree_basis(gram, blocks)
     part = jnp.einsum("ab,ax->bx", basis, flat.astype(jnp.float32), precision=HIGH).reshape(
         RANK, rows, -1

time: 412 us -> 344 us (0.83)
  waiting for transfers between devices: 274 us -> 181 us
  blocking collectives: 17.1 us -> 51.5 us
  starting transfers between devices: 12.6 us -> 4.18 us
    psum x1 -> x2, waiting for transfers between devices: 245 us -> 180 us  [local(): gram = lax.psum(gram, name)]
    all_to_all x0 -> x1, blocking collectives: none -> 37 us  [local(): cells = lax.all_to_all(vorticity, 'tm', 2, 0, tiled=True)]
    all_to_all x1 -> x0, waiting for transfers between devices: 28.5 us -> none  [local(): cells = lax.all_to_all(vorticity, 'tm', 2, 0, tiled=True)]
    all_to_all x1 -> x0, starting transfers between devices: 8.47 us -> none  [local(): cells = lax.all_to_all(vorticity, 'tm', 2, 0, tiled=True)]
where the time goes in v1:
time: 344 us; the launch traced here: 343 us
  waiting for transfers between devices  181 us (53%)
  blocking collectives  51.5 us (15%)
  other arithmetic  44.8 us (13%)
  local copies, waits for them, and re-layouts  37.1 us (11%)
  between operations  14.4 us (4%)
  matrix products  10.4 us (3%)
  starting transfers between devices  4.18 us (1%)
    psum x2, waiting for transfers between devices, local(): gram = lax.psum(gram, name)  180 us
    all_to_all x1, blocking collectives, local(): cells = lax.all_to_all(vorticity, 'tm', 2, 0, tiled=True)  37 us
    another operation x9, other arithmetic, merge_small(): lower = jnp.linalg.cholesky(inner)  21.5 us
    another operation x7, other arithmetic, merge_small(): lax.linalg.triangular_solve(lower, eye, left_side=True, lower=True)  18 us
    all_to_all x1, blocking collectives, local(): modes = lax.all_to_all(part, 'tm', 0, 2, tiled=True)  14.4 us
    unnamed x8, local copies, waits for them, and re-layouts  12.4 us
  transfers between devices with their start and end apart: 4, of which 3 were waited for; matrix products, arithmetic and copies ran while one was open for 1% of the time, Pallas kernels for 0%

profile of v1, /device:TPU:2, one launch (start us, length us, event | category | flops | bytes accessed | tf_op | source)
XLA Modules:
  0.0 343.2 jit_solution(257742224501949670)
XLA Ops:
  7.2 1.9 bitcast_convert_fusion
  9.1 0.6 copy.179
  9.8 3.8 %collective-permute-start.1 = (bf16[32,2,1024]{2,0,1:T(8,128)(2,1)S(1)}, bf16[32,2,1024]{2,0,1:T(8,128)(2,1)S(1)}, u32[]{:S(2)}, u32[]{:S(2)}) collective-permute-start(bf16[32,2,1024]{2,0,1:T(8,128)(2,1)S(1)} %get-tuple-element.19), channel_id=1, source_target_pairs={{8,0},{16,8},{24,16},{32,24},{40,32},{48,40},{56,48},{64,56},{72,6... | collective-permute-start | bytes 393224 | tf_op jit(solution)/shard_map/ppermute | solution.py:16
  13.6 0.7 fusion.72
  14.4 0.7 fusion.74
  15.4 0.8 collective-permute-done
  16.4 0.8 copy_convert_fusion
  17.2 2.2 fusion.3
  19.5 5.1 %copy.130 = bf16[32,16,1024]{0,1,2:T(8,128)(2,1)} copy(bf16[32,16,1024]{2,1,0:T(8,128)(2,1)S(1)} %fusion.3) | data formatting | bytes 2097152 | tf_op jit(solution)/shard_map/convert_element_type | solution.py:82
  24.6 7.0 %reshape.157 = bf16[8,2,32768]{2,1,0:T(2,128)(2,1)S(1)} reshape(bf16[1024,16,32]{2,1,0:T(8,128)(2,1)} %bitcast.133) | data formatting | bytes 2097152
  31.6 37.0 %all_to_all.33 = bf16[8,2,32768]{2,1,0:T(2,128)(2,1)S(1)} all-to-all(bf16[8,2,32768]{2,1,0:T(2,128)(2,1)S(1)} %reshape.157), channel_id=1, replica_groups=mesh['space'=32,'tm'=8] {'tm'}, dimensions={0} | all-to-all | bytes 2097152 | tf_op jit(solution)/shard_map/all_to_all | solution.py:84
  68.6 4.5 %reshape.158 = bf16[1024,16,32]{2,1,0:T(8,128)(2,1)} reshape(bf16[8,2,32768]{2,1,0:T(2,128)(2,1)S(1)} %all_to_all.33) | data formatting | bytes 2097152
  73.1 5.4 %copy.131 = bf16[32,16,8,128]{3,1,0,2:T(8,128)(2,1)S(1)} copy(bf16[32,16,8,128]{0,1,3,2:T(8,128)(2,1)} %bitcast.132) | data formatting | bytes 2097152 | tf_op jit(solution)/shard_map/all_to_all | solution.py:84
  78.5 1.2 fusion.10
  79.9 106.4 %all-reduce.7.cloned.1.call-done = f32[256,256]{0,1:T(8,128)} async-done(((f32[256,256]{0,1:T(8,128)}), f32[256,256]{0,1:T(8,128)}) %all-reduce.7.cloned.1.call-update) | async-done | bytes 262160 | tf_op jit(solution)/shard_map/psum | solution.py:88
  186.4 0.7 copy.133
  187.1 0.3 copy.178
  187.3 0.5 copy.152
  187.9 73.6 %all-reduce.9.cloned.1.call-done = f32[256,256]{0,1:T(8,128)} async-done(((f32[256,256]{0,1:T(8,128)}), f32[256,256]{0,1:T(8,128)}) %all-reduce.9.cloned.1.call-update) | async-done | bytes 262160 | tf_op jit(solution)/shard_map/psum | solution.py:88
  261.5 0.9 slice_bitcast_fusion.7
  262.4 1.9 copy.137
  264.3 0.9 fusion.70
  265.2 1.5 gather_fusion
  266.6 0.8 copy.138
  267.5 1.1 fusion.69
  268.7 11.7 %custom-call.21 = f32[4,32,32]{2,1,0:T(8,128)S(1)} custom-call(f32[4,32,32]{2,1,0:T(8,128)S(1)} %fusion.19), custom_call_target="Cholesky" | custom-call | tf_op jit(solution)/shard_map/jit(cholesky)/cholesky | solution.py:34
  280.7 9.8 %custom-call.22 = f32[4,1,32,32]{2,3,1,0:T(8,128)S(1)} custom-call(f32[4,1,32,32]{3,2,1,0:T(8,128)S(1)} %select_bitcast_fusion), custom_call_target="InvertDiagBlocksLowerTriangular" | custom-call | tf_op jit(solution)/shard_map/triangular_solve | solution.py:36
  290.5 0.9 convolution_multiply_fusion
  291.5 0.3 fusion.68
  291.8 0.3 fusion.13
  292.1 0.3 fusion.39
  292.4 1.9 copy.147
  294.3 0.8 fusion.67
  295.1 1.5 gather_fusion.1
  296.6 0.8 copy.148
  297.5 0.9 fusion.66
  298.6 5.9 %custom-call.23 = f32[2,32,32]{2,1,0:T(8,128)S(1)} custom-call(f32[2,32,32]{2,1,0:T(8,128)S(1)} %fusion.32), custom_call_target="Cholesky" | custom-call | tf_op jit(solution)/shard_map/jit(cholesky)/cholesky | solution.py:34
  304.7 4.9 %custom-call.24 = f32[2,1,32,32]{2,3,1,0:T(8,128)S(1)} custom-call(f32[2,1,32,32]{3,2,1,0:T(8,128)S(1)} %select_bitcast_fusion.1), custom_call_target="InvertDiagBlocksLowerTriangular" | custom-call | tf_op jit(solution)/shard_map/triangular_solve | solution.py:36
  309.6 0.9 convolution_multiply_fusion.1
  311.0 0.3 fusion.23
  311.5 0.8 gather_fusion.2
  312.7 2.9 custom-call.25
  315.6 0.6 compare_reduce_fusion
  316.3 0.7 fusion.34
  316.9 2.4 custom-call.26
  320.0 1.0 fusion.76
  321.2 14.4 %all_to_all.34 = f32[32,16,128]{2,1,0:T(8,128)S(1)} all-to-all(f32[32,16,128]{2,1,0:T(8,128)S(1)} %copy.153), channel_id=1, replica_groups=mesh['space'=32,'tm'=8] {'tm'}, dimensions={0} | all-to-all | bytes 524288 | tf_op jit(solution)/shard_map/all_to_all | solution.py:93
  335.6 0.7 copy.180
  (47 shorter events, 3.6 us)
Async XLA Ops:
  7.2 179.2 %all-reduce.7.cloned.1.call-start = ((), (), s32[]{:S(2)}) async-start(), calls=%async_computation.2 | async-start | bytes 524288 | tf_op jit(solution)/shard_map/psum | solution.py:88
  9.7 6.6 %collective-permute-start = (bf16[32,2,1024]{2,0,1:T(8,128)(2,1)S(1)}, bf16[32,2,1024]{2,0,1:T(8,128)(2,1)S(1)}, u32[]{:S(2)}, u32[]{:S(2)}) collective-permute-start(bf16[32,2,1024]{2,0,1:T(8,128)(2,1)S(1)} %get-tuple-element.18), channel_id=1, source_target_pairs={{0,8},{8,16},{16,24},{24,32},{32,40},{40,48},{48,56},{56,64},{64,7... | collective-permute-start | bytes 393224 | tf_op jit(solution)/shard_map/ppermute | solution.py:15
  9.8 6.5 %collective-permute-start.1 = (bf16[32,2,1024]{2,0,1:T(8,128)(2,1)S(1)}, bf16[32,2,1024]{2,0,1:T(8,128)(2,1)S(1)}, u32[]{:S(2)}, u32[]{:S(2)}) collective-permute-start(bf16[32,2,1024]{2,0,1:T(8,128)(2,1)S(1)} %get-tuple-element.19), channel_id=1, source_target_pairs={{8,0},{16,8},{24,16},{32,24},{40,32},{48,40},{56,48},{64,56},{72,6... | collective-permute-start | bytes 393224 | tf_op jit(solution)/shard_map/ppermute | solution.py:16
  19.5 5.1 %copy-start = (bf16[32,16,1024]{2,1,0:T(8,128)(2,1)}, bf16[32,16,1024]{2,1,0:T(8,128)(2,1)S(1)}, u32[]{:S(2)}) copy-start(bf16[32,16,1024]{2,1,0:T(8,128)(2,1)S(1)} %fusion.3) | copy-start | bytes 3145732
  79.7 181.8 %all-reduce.9.cloned.1.call-start = ((), (), s32[]{:S(2)}) async-start(), calls=%async_computation.3 | async-start | bytes 524288 | tf_op jit(solution)/shard_map/psum | solution.py:88
  262.3 29.5 %copy-start.1 = (f32[256,256]{0,1:T(8,128)S(1)}, f32[256,256]{0,1:T(8,128)}, u32[]{:S(2)}) copy-start(f32[256,256]{0,1:T(8,128)} %all-reduce.9.cloned.1.call-done) | copy-start | bytes 786436
Sparse Core Ops, SparseCore 0:
  79.8 106.4 all-reduce.6
  188.8 72.6 all-reduce.8
